TPU v7x, 32 devices: a whole 2x2x4 slice. The times are simulated.
32 devices in a mesh: px: 8 (over z, x), py: 4 (over y, core).
Axes of the slice: x: 2, y: 2, z: 4, core: 2. Of those that a mesh axis runs over, the one named last changes fastest.
Arguments:
- conserved: float32 [2, 2, 2, 2, 32, 32, 128], P(None, None, None, None, 'px', 'py'), may hold values from 0.075 to 36
- velocity: float32 [3, 3, 3, 3, 32, 32, 128], P(None, None, None, None, 'px', 'py'), may hold values from -6 to 6
- targets: float32 [2], replicated, may hold values from 0.5 to 2
- handoff_blocks: int32 [8, 32], P('px', 'py'), may hold values from 0 to 31, as said below
- handoff_owner: int32 [8, 32, 1], P('px', 'py'), may hold values from 0 to 3; in each aligned block of 8 rows (0 to 7, 8 to 15, ..., all dimensions but the last counted through in order) at most 4 rows name the same one
Outputs:
- fixed_state: float32 [2, 2, 2, 2, 32, 32, 128], P(None, None, None, None, 'px', 'py')
- handed: float32 [8, 64, 16, 128], P('px', 'py')
Inputs may be any that keep to these rules, and one draw needn't show every extreme that they name: `handoff_blocks`: within one device's 8 entries the column numbers are distinct; column b is the local zone column (b // 8, b % 8). `handoff_owner`: owners are indices along py within the same px group; at most 4 of one device's entries name the same owner, and in some device one owner is named exactly 4 times.
All inputs are finite; a program needn't handle non-finite values.
Results may differ from a plain program's by a relative error of at most 0.00035.
Values sent between devices are 32-bit elements; how exact they have to be, the bound alone decides.
No kernel may reach another device: no remote copies, remote signals or barrier semaphores. Data moves between devices by JAX's collectives and lax.ppermute only.
A program may use at most 64 MiB of HBM per device.

v0:
```python
import math
import jax
import jax.numpy as jnp
import numpy as np
from jax import lax
from jax.sharding import PartitionSpec as P

gamma_less = 0.4
force_step = 0.02
advect_step = 0.5
highest = lax.Precision.HIGHEST


def passed_along(x, axis, by):
    size = lax.axis_size(axis)
    pairs = [(i, i + by) for i in range(size) if 0 <= i + by < size]
    return lax.ppermute(x, axis, pairs)


def triple(factor_one, factor_two, factor_three):
    return np.kron(np.kron(factor_one, factor_two), factor_three)


def build_tables():
    offset = 0.5 / math.sqrt(3.0)
    gauss_nodes = np.array([0.5 - offset, 0.5 + offset])
    linear = np.stack([1.0 - gauss_nodes, gauss_nodes], 1)
    quadratic = np.stack(
        [
            2.0 * (gauss_nodes - 0.5) * (gauss_nodes - 1.0),
            -4.0 * gauss_nodes * (gauss_nodes - 1.0),
            2.0 * gauss_nodes * (gauss_nodes - 0.5),
        ],
        1,
    )
    slopes = np.stack(
        [4.0 * gauss_nodes - 3.0, 4.0 - 8.0 * gauss_nodes, 4.0 * gauss_nodes - 1.0], 1
    )
    line_mass = np.array([[1.0 / 3.0, 1.0 / 6.0], [1.0 / 6.0, 1.0 / 3.0]])
    line_inverse = np.array([[4.0, -2.0], [-2.0, 4.0]])
    line_drift = np.array([[-0.5, -0.5], [0.5, 0.5]])
    basis = triple(linear, linear, linear)
    gradient = np.stack(
        [
            triple(slopes, quadratic, quadratic),
            triple(quadratic, slopes, quadratic),
            triple(quadratic, quadratic, slopes),
        ],
        1,
    ).reshape(8, 81)
    inverse = triple(line_inverse, line_inverse, line_inverse)
    project = inverse @ basis.T / 8.0
    stiffness = np.stack(
        [
            triple(line_drift, line_mass, line_mass),
            triple(line_mass, line_drift, line_mass),
            triple(line_mass, line_mass, line_drift),
        ]
    )
    face_mass = np.kron(line_mass, line_mass)
    return tuple(
        (
            jnp.asarray(entry_table, jnp.float32)
            for entry_table in (basis, gradient, inverse, project, stiffness, face_mass)
        )
    )


def face_weight(fluxes, face_mass):
    layout = fluxes.shape
    grouped = fluxes.reshape(layout[0], 4, -1)
    return jnp.einsum("ab,fbn->fan", face_mass, grouped, precision=highest).reshape(layout)


def upwind(left_trace, right_trace, speeds, face_mass):
    fluxes = 0.5 * speeds * (left_trace + right_trace) + 0.5 * jnp.abs(speeds) * (
        left_trace - right_trace
    )
    return face_weight(fluxes, face_mass)


def lagrange_section(conserved, velocity, tables):
    basis, gradient, inverse, project, stiffness, face_mass = tables
    layout = conserved.shape
    zone_count = layout[4] * layout[5] * layout[6]
    fields = conserved.reshape(2, 8, zone_count)
    node_motion = velocity.reshape(81, zone_count)
    divergence = jnp.dot(gradient, node_motion, precision=highest)
    pressure = gamma_less * jnp.dot(basis, fields[1], precision=highest)
    energy = fields[1] - force_step * jnp.dot(project, pressure * divergence, precision=highest)
    lagrange = jnp.stack([fields[0], energy]).reshape(layout)
    mean_motion = jnp.sum(velocity.reshape(3, 27, layout[4], layout[5], layout[6]), axis=1) / 27.0
    padded = jnp.pad(mean_motion, ((0, 0), (0, 0), (0, 0), (1, 1)))
    relaxed = 0.25 * (padded[..., :-2] + 2.0 * mean_motion + padded[..., 2:])
    return (lagrange, mean_motion - relaxed)


def advect(lagrange, relative, x_faces, y_faces, tables):
    basis, gradient, inverse, project, stiffness, face_mass = tables
    layout = lagrange.shape
    zone_count = layout[4] * layout[5] * layout[6]
    flat_state = lagrange.reshape(2, 8, zone_count)
    volume = jnp.zeros_like(flat_state)
    for direction in range(3):
        volume = volume + jnp.einsum(
            "jk,fkn->fjn", stiffness[direction], flat_state, precision=highest
        ) * relative[direction].reshape(1, 1, zone_count)
    padded_z = jnp.pad(lagrange, ((0, 0),) * 6 + ((1, 1),))
    motion_z = jnp.pad(relative[2], ((0, 0), (0, 0), (1, 1)))
    flux_z = upwind(
        padded_z[:, :, :, 1, :, :, :-1],
        padded_z[:, :, :, 0, :, :, 1:],
        0.5 * (motion_z[..., :-1] + motion_z[..., 1:]),
        face_mass,
    )
    face_z = jnp.stack([-flux_z[..., :-1], flux_z[..., 1:]], axis=3)
    flux_x = upwind(x_faces[0], x_faces[1], x_faces[2], face_mass)
    face_x = jnp.stack([-flux_x[:, :, :, :-1], flux_x[:, :, :, 1:]], axis=1)
    flux_y = upwind(y_faces[0], y_faces[1], y_faces[2], face_mass)
    face_y = jnp.stack([-flux_y[:, :, :, :, :-1], flux_y[:, :, :, :, 1:]], axis=2)
    balance = volume - (face_x + face_y + face_z).reshape(2, 8, zone_count)
    remapped = flat_state + advect_step * jnp.einsum(
        "jk,fkn->fjn", inverse, balance, precision=highest
    )
    return remapped.reshape(layout)


def body(conserved, velocity, targets, handoff_blocks, handoff_owner):
    tables = build_tables()
    lagrange, relative = lagrange_section(conserved, velocity, tables)
    width_x = lagrange.shape[4]
    width_y = lagrange.shape[5]
    depth_z = lagrange.shape[6]
    count_px = lax.axis_size("px")
    count_py = lax.axis_size("py")
    total_zones = 8.0 * width_x * width_y * depth_z * count_px * count_py
    upper_x = jnp.concatenate(
        [lagrange[:, 1, :, :, -1].reshape((8, width_y, depth_z)), relative[0, -1][None]], axis=0
    )
    lower_x = jnp.concatenate(
        [lagrange[:, 0, :, :, 0].reshape((8, width_y, depth_z)), relative[0, 0][None]], axis=0
    )
    below_x = passed_along(upper_x, "px", 1)
    above_x = passed_along(lower_x, "px", -1)
    left_x = jnp.concatenate(
        [below_x[:8].reshape((2, 2, 2, 1, width_y, depth_z)), lagrange[:, 1]], axis=3
    )
    right_x = jnp.concatenate(
        [lagrange[:, 0], above_x[:8].reshape((2, 2, 2, 1, width_y, depth_z))], axis=3
    )
    motion_x = jnp.concatenate([below_x[8][None], relative[0], above_x[8][None]], axis=0)
    x_faces = (left_x, right_x, 0.5 * (motion_x[:-1] + motion_x[1:]))
    upper_y = jnp.concatenate(
        [lagrange[:, :, 1, :, :, -1].reshape((8, width_x, depth_z)), relative[1][:, -1][None]],
        axis=0,
    )
    lower_y = jnp.concatenate(
        [lagrange[:, :, 0, :, :, 0].reshape((8, width_x, depth_z)), relative[1][:, 0][None]], axis=0
    )
    below_y = passed_along(upper_y, "py", 1)
    above_y = passed_along(lower_y, "py", -1)
    left_y = jnp.concatenate(
        [below_y[:8].reshape((2, 2, 2, width_x, 1, depth_z)), lagrange[:, :, 1]], axis=4
    )
    right_y = jnp.concatenate(
        [lagrange[:, :, 0], above_y[:8].reshape((2, 2, 2, width_x, 1, depth_z))], axis=4
    )
    motion_y = jnp.concatenate([below_y[8][:, None], relative[1], above_y[8][:, None]], axis=1)
    y_faces = (left_y, right_y, 0.5 * (motion_y[:, :-1] + motion_y[:, 1:]))
    remapped = advect(lagrange, relative, x_faces, y_faces, tables)
    totals = lax.psum(jnp.sum(remapped.reshape(2, -1), axis=1), ("px", "py"))
    field_means = totals / total_zones
    fixed_state = remapped * (targets / field_means).reshape(2, 1, 1, 1, 1, 1, 1)
    entries = handoff_blocks.shape[1]
    capacity = max(2, 2 * entries // count_py)
    blocks = handoff_blocks[0]
    owners = handoff_owner[0, :, 0]
    onehot = (owners[:, None] == jnp.arange(count_py, dtype=jnp.int32)).astype(jnp.int32)
    earlier = jnp.cumsum(onehot, axis=0) - onehot
    slot_index = jnp.sum(onehot * earlier, axis=1)
    position = owners * capacity + slot_index
    placing = (
        position[None, :] == jnp.arange(count_py * capacity, dtype=jnp.int32)[:, None]
    ).astype(jnp.float32)
    columns = fixed_state.reshape((16, width_x * width_y, depth_z))
    picked = jnp.take(columns, blocks, axis=1)
    send_rows = jnp.einsum("sn,cnz->scz", placing, picked, precision=highest).reshape(
        (count_py, capacity, 16, depth_z)
    )
    received = lax.all_to_all(send_rows, "py", split_axis=0, concat_axis=0, tiled=True)
    handed = received.reshape((1, count_py * capacity, 16, depth_z))
    return (fixed_state, handed)


def solution(mesh):
    return jax.shard_map(
        body,
        mesh=mesh,
        in_specs=(
            P(None, None, None, None, "px", "py", None),
            P(None, None, None, None, "px", "py", None),
            P(),
            P("px", "py"),
            P("px", "py", None),
        ),
        out_specs=(P(None, None, None, None, "px", "py", None), P("px", "py", None, None)),
        check_vma=False,
    )
```

profile of v0, /device:TPU:0, one launch (start us, length us, event | category | flops | bytes accessed | tf_op | source)
XLA Modules:
  0.0 75.8 jit_solution(11837693475548157601)
XLA Ops:
  0.6 1.0 %fusion.62 = (f32[1,2,2,2,4,8,128]{6,5,4,3,2,1,0:T(8,128)S(1)}, f32[1,2,2,2,4,8,128]{6,5,4,3,2,1,0:T(8,128)S(1)}) fusion(f32[2,2,2,2,4,8,128]{6,5,4,3,2,1,0:T(8,128)} %param.11), kind=kLoop, calls=%fused_computation.139 | loop fusion | bytes 524288 | tf_op jit(solution)/shard_map/slice | solution.py:90
  1.7 1.5 %reshape.163 = f32[81,4096]{1,0:T(8,128)S(1)} reshape(f32[3,3,3,3,4,8,128]{6,5,4,3,2,1,0:T(8,128)} %param.12) | data formatting | bytes 2654208 | tf_op jit(solution)/shard_map/reshape | solution.py:87
  3.5 0.8 %convolution_multiply_fusion.5 = f32[8,4096]{1,0:T(8,128)S(1)} fusion(f32[8,4096]{1,0:T(8,128)S(1)} %convolution_multiply_fusion.6, f32[8,81]{1,0:T(8,128)S(1)} %copy-done.8, f32[81,4096]{1,0:T(8,128)S(1)} %reshape.163), kind=kOutput, calls=%fused_computation.17 | convolution fusion | flops 31883264 | bytes 1591840 | tf_op jit(solution)/shard_map/dot_general | solution.py:88
  4.9 2.4 %collective-permute-start.2 = (f32[9,4,128]{2,1,0:T(4,128)S(1)}, f32[9,4,128]{2,1,0:T(4,128)S(1)}, u32[]{:S(2)}, u32[]{:S(2)}) collective-permute-start(f32[9,4,128]{2,1,0:T(4,128)S(1)} %pad_maximum_fusion.11), channel_id=1, source_target_pairs={{0,1},{1,2},{2,3},{4,5},{5,6},{6,7},{8,9},{9,10},{10,11},{12,13},{... | collective-permute-start | bytes 55304 | tf_op jit(solution)/shard_map/ppermute | solution.py:17
  7.4 1.3 %collective-permute-start.3 = (f32[9,4,128]{2,1,0:T(4,128)S(1)}, f32[9,4,128]{2,1,0:T(4,128)S(1)}, u32[]{:S(2)}, u32[]{:S(2)}) collective-permute-start(f32[9,4,128]{2,1,0:T(4,128)S(1)} %pad_maximum_fusion.12), channel_id=1, source_target_pairs={{1,0},{2,1},{3,2},{5,4},{6,5},{7,6},{9,8},{10,9},{11,10},{13,12},{... | collective-permute-start | bytes 55304 | tf_op jit(solution)/shard_map/ppermute | solution.py:17
  8.7 4.2 %collective-permute-start = (f32[9,8,128]{2,1,0:T(8,128)S(1)}, f32[9,8,128]{2,1,0:T(8,128)S(1)}, u32[]{:S(2)}, u32[]{:S(2)}) collective-permute-start(f32[9,8,128]{2,1,0:T(8,128)S(1)} %pad_maximum_fusion.9), channel_id=1, source_target_pairs={{0,4},{4,8},{8,12},{12,16},{16,20},{20,24},{24,28},{1,5},{5,9},{9,... | collective-permute-start | bytes 110600 | tf_op jit(solution)/shard_map/ppermute | solution.py:17
  12.9 1.3 %collective-permute-start.1 = (f32[9,8,128]{2,1,0:T(8,128)S(1)}, f32[9,8,128]{2,1,0:T(8,128)S(1)}, u32[]{:S(2)}, u32[]{:S(2)}) collective-permute-start(f32[9,8,128]{2,1,0:T(8,128)S(1)} %pad_maximum_fusion.10), channel_id=1, source_target_pairs={{4,0},{8,4},{12,8},{16,12},{20,16},{24,20},{28,24},{5,1},{9,5},{13... | collective-permute-start | bytes 110600 | tf_op jit(solution)/shard_map/ppermute | solution.py:17
  15.5 0.4 convolution_bitcast_fusion
  16.5 0.3 convolution_multiply_fusion.3
  16.9 0.4 fusion.5
  17.6 0.4 convolution_bitcast_fusion.1
  18.2 0.6 collective-permute-done.1
  19.0 0.4 convolution_bitcast_fusion.2
  19.8 0.5 copy-done.3
  20.2 0.4 fusion.4
  20.6 0.4 fusion.65
  21.1 43.9 %psum.7 = f32[2]{0:T(128)S(1)} all-reduce(f32[2]{0:T(128)S(1)} %get-tuple-element.40), channel_id=1, replica_groups=mesh['px'=8,'py'=4] {'px','py'}, use_global_device_ids=true, to_apply=%region_2.3 | all-reduce | flops 2 | bytes 16 | tf_op jit(solution)/shard_map/psum | solution.py:171
  65.4 0.6 gather_fusion
  66.0 0.3 fusion.41
  66.4 0.7 copy.106
  67.0 3.5 %all-to-all-start = ((f32[4,4,16,128]{3,1,2,0:T(4,128)}), f32[4,4,16,128]{3,1,2,0:T(4,128)S(1)}, u32[]{:S(2)}, u32[]{:S(2)}) async-start(f32[4,4,16,128]{3,1,2,0:T(4,128)} %copy.106), calls=%async_computation | async-start | bytes 262144 | tf_op jit(solution)/shard_map/all_to_all | solution.py:190
  70.6 0.8 %broadcast_multiply_fusion = f32[2,2,2,2,4,8,128]{6,5,4,3,2,1,0:T(8,128)} fusion(f32[2,2,2,2,4,8,128]{6,5,4,3,2,1,0:T(8,128)S(1)} %bitcast.158, f32[2]{0:T(128)S(1)} %multiply_divide_fusion), kind=kLoop, calls=%fused_computation.78 | loop fusion | flops 65536 | bytes 524296 | tf_op jit(solution)/shard_map/mul | solution.py:173
  71.4 3.8 %all-to-all-done = f32[4,4,16,128]{3,1,2,0:T(4,128)S(1)} async-done(((f32[4,4,16,128]{3,1,2,0:T(4,128)}), f32[4,4,16,128]{3,1,2,0:T(4,128)S(1)}, u32[]{:S(2)}, u32[]{:S(2)}) %all-to-all-start) | async-done | bytes 131104 | tf_op jit(solution)/shard_map/all_to_all | solution.py:190
  75.2 0.7 copy.107
  (94 shorter events, 3.8 us)
Async XLA Ops:
  1.7 1.6 %copy-start.6 = (f32[8,8]{1,0:T(8,128)S(1)}, f32[8,8]{1,0:T(8,128)}, u32[]{:S(2)}) copy-start(f32[8,8]{1,0:T(8,128)} %constant.61.clone) | copy-start | bytes 772
  1.7 1.9 %copy-start.8 = (f32[8,81]{1,0:T(8,128)S(1)}, f32[8,81]{1,0:T(8,128)}, u32[]{:S(2)}) copy-start(f32[8,81]{1,0:T(8,128)} %constant.62.clone) | copy-start | bytes 7780
  3.2 1.1 %copy-start.7 = (f32[8,8]{1,0:T(8,128)S(1)}, f32[8,8]{1,0:T(8,128)}, u32[]{:S(2)}) copy-start(f32[8,8]{1,0:T(8,128)} %constant.64.clone) | copy-start | bytes 772
  3.3 1.4 %copy-start = (f32[3,3,3,3,4,8,128]{6,5,4,3,2,1,0:T(8,128)S(1)}, f32[3,3,3,3,4,8,128]{6,5,4,3,2,1,0:T(8,128)}, u32[]{:S(2)}) copy-start(f32[3,3,3,3,4,8,128]{6,5,4,3,2,1,0:T(8,128)} %param.12) | copy-start | bytes 3981316
  4.8 9.5 %copy-start.10 = (s32[1,8]{1,0:T(1,128)S(1)}, s32[1,8]{1,0:T(1,128)}, u32[]{:S(2)}) copy-start(s32[1,8]{1,0:T(1,128)} %param.14) | copy-start | bytes 100
  4.9 12.3 %collective-permute-start.2 = (f32[9,4,128]{2,1,0:T(4,128)S(1)}, f32[9,4,128]{2,1,0:T(4,128)S(1)}, u32[]{:S(2)}, u32[]{:S(2)}) collective-permute-start(f32[9,4,128]{2,1,0:T(4,128)S(1)} %pad_maximum_fusion.11), channel_id=1, source_target_pairs={{0,1},{1,2},{2,3},{4,5},{5,6},{6,7},{8,9},{9,10},{10,11},{12,13},{... | collective-permute-start | bytes 55304 | tf_op jit(solution)/shard_map/ppermute | solution.py:17
  7.4 9.9 %collective-permute-start.3 = (f32[9,4,128]{2,1,0:T(4,128)S(1)}, f32[9,4,128]{2,1,0:T(4,128)S(1)}, u32[]{:S(2)}, u32[]{:S(2)}) collective-permute-start(f32[9,4,128]{2,1,0:T(4,128)S(1)} %pad_maximum_fusion.12), channel_id=1, source_target_pairs={{1,0},{2,1},{3,2},{5,4},{6,5},{7,6},{9,8},{10,9},{11,10},{13,12},{... | collective-permute-start | bytes 55304 | tf_op jit(solution)/shard_map/ppermute | solution.py:17
  8.7 9.4 %collective-permute-start = (f32[9,8,128]{2,1,0:T(8,128)S(1)}, f32[9,8,128]{2,1,0:T(8,128)S(1)}, u32[]{:S(2)}, u32[]{:S(2)}) collective-permute-start(f32[9,8,128]{2,1,0:T(8,128)S(1)} %pad_maximum_fusion.9), channel_id=1, source_target_pairs={{0,4},{4,8},{8,12},{12,16},{16,20},{20,24},{24,28},{1,5},{5,9},{9,... | collective-permute-start | bytes 110600 | tf_op jit(solution)/shard_map/ppermute | solution.py:17
  12.9 5.9 %collective-permute-start.1 = (f32[9,8,128]{2,1,0:T(8,128)S(1)}, f32[9,8,128]{2,1,0:T(8,128)S(1)}, u32[]{:S(2)}, u32[]{:S(2)}) collective-permute-start(f32[9,8,128]{2,1,0:T(8,128)S(1)} %pad_maximum_fusion.10), channel_id=1, source_target_pairs={{4,0},{8,4},{12,8},{16,12},{20,16},{24,20},{28,24},{5,1},{9,5},{13... | collective-permute-start | bytes 110600 | tf_op jit(solution)/shard_map/ppermute | solution.py:17
  14.3 1.2 %copy-start.1 = (f32[4,4,1]{1,0,2:T(4,128)S(1)}, f32[4,4,1]{1,0,2:T(4,128)}, u32[]{:S(2)}) copy-start(f32[4,4,1]{1,0,2:T(4,128)} %constant.86) | copy-start | bytes 196
  14.4 1.9 %copy-start.9 = (s32[1,8,1]{1,2,0:T(1,128)S(1)}, s32[1,8,1]{1,2,0:T(1,128)}, u32[]{:S(2)}) copy-start(s32[1,8,1]{1,2,0:T(1,128)} %param.15) | copy-start | bytes 100
  14.6 1.9 %copy-start.5 = (f32[8,8,1]{1,0,2:T(8,128)S(1)}, f32[8,8,1]{1,0,2:T(8,128)}, u32[]{:S(2)}) copy-start(f32[8,8,1]{1,0,2:T(8,128)} %constant.83) | copy-start | bytes 772
  14.9 2.0 %copy-start.4 = (f32[8,8,1]{1,0,2:T(8,128)S(1)}, f32[8,8,1]{1,0,2:T(8,128)}, u32[]{:S(2)}) copy-start(f32[8,8,1]{1,0,2:T(8,128)} %constant.84) | copy-start | bytes 772
  19.5 0.7 copy-start.3
  19.6 1.0 %copy-start.2 = (f32[8,8,1]{1,0,2:T(8,128)S(1)}, f32[8,8,1]{1,0,2:T(8,128)}, u32[]{:S(2)}) copy-start(f32[8,8,1]{1,0,2:T(8,128)} %constant.87) | copy-start | bytes 772
  19.7 45.4 %copy-start.11 = (f32[2]{0:T(128)S(1)}, f32[2]{0:T(128)}, u32[]{:S(2)}) copy-start(f32[2]{0:T(128)} %param.13) | copy-start | bytes 28
  67.0 8.1 %all-to-all-start = ((f32[4,4,16,128]{3,1,2,0:T(4,128)}), f32[4,4,16,128]{3,1,2,0:T(4,128)S(1)}, u32[]{:S(2)}, u32[]{:S(2)}) async-start(f32[4,4,16,128]{3,1,2,0:T(4,128)} %copy.106), calls=%async_computation | async-start | bytes 262144 | tf_op jit(solution)/shard_map/all_to_all | solution.py:190
where the time goes:
time: 76.3 us; the launch traced here: 75.8 us
  blocking collectives  43.9 us (58%)
  starting transfers between devices  12.7 us (17%)
  local copies, waits for them, and re-layouts  6.92 us (9%)
  waiting for transfers between devices  4.44 us (6%)
  matrix products  4.35 us (6%)
  other arithmetic  2.08 us (3%)
  between operations  1.39 us (2%)
    psum x1, blocking collectives, body(): totals = lax.psum(jnp.sum(remapped.reshape(2, -1), axis=1), ('px', 'py'))  43.9 us
    ppermute x4, starting transfers between devices, passed_along(): return lax.ppermute(x, axis, pairs)  9.2 us
    all_to_all x1, waiting for transfers between devices, body(): lax.all_to_all(send_rows, 'py', split_axis=0, concat_axis=0, tiled=True)  3.81 us
    all_to_all x1, starting transfers between devices, body(): lax.all_to_all(send_rows, 'py', split_axis=0, concat_axis=0, tiled=True)  3.54 us
    reshape x1, local copies, waits for them, and re-layouts, lagrange_section(): node_motion = velocity.reshape(81, zone_count)  1.54 us
  transfers between devices with their start and end apart: 5, of which 2 were waited for; matrix products, arithmetic and copies ran while one was open for 6% of the time, Pallas kernels for 0%

commit v1 on v0

--- a/solution.py
+++ b/solution.py
@@ -168,7 +168,9 @@
     motion_y = jnp.concatenate([below_y[8][:, None], relative[1], above_y[8][:, None]], axis=1)
     y_faces = (left_y, right_y, 0.5 * (motion_y[:, :-1] + motion_y[:, 1:]))
     remapped = advect(lagrange, relative, x_faces, y_faces, tables)
-    totals = lax.psum(jnp.sum(remapped.reshape(2, -1), axis=1), ("px", "py"))
+    value = jnp.sum(remapped.reshape(2, -1), axis=1)
+    pieces = lax.all_gather(value, ("px", "py"))
+    totals = jnp.sum(pieces, axis=0)
     field_means = totals / total_zones
     fixed_state = remapped * (targets / field_means).reshape(2, 1, 1, 1, 1, 1, 1)
     entries = handoff_blocks.shape[1]

time: 76.3 us -> 76.6 us (level)
    psum x1 -> x0, blocking collectives: 43.9 us -> none  [body(): totals = lax.psum(jnp.sum(remapped.reshape(2, -1), axis=1), ('px', 'py'))]
    unnamed x0 -> x1, blocking collectives: none -> 43.9 us
where the time goes in v1:
time: 76.6 us; the launch traced here: 76.2 us
  blocking collectives  43.9 us (57%)
  starting transfers between devices  12.7 us (17%)
  local copies, waits for them, and re-layouts  7.25 us (9%)
  waiting for transfers between devices  4.43 us (6%)
  matrix products  4.35 us (6%)
  other arithmetic  2.1 us (3%)
  between operations  1.42 us (2%)
    unnamed x1, blocking collectives  43.9 us
    ppermute x4, starting transfers between devices, passed_along(): return lax.ppermute(x, axis, pairs)  9.2 us
    all_to_all x1, waiting for transfers between devices, body(): lax.all_to_all(send_rows, 'py', split_axis=0, concat_axis=0, tiled=True)  3.81 us
    all_to_all x1, starting transfers between devices, body(): lax.all_to_all(send_rows, 'py', split_axis=0, concat_axis=0, tiled=True)  3.54 us
    reshape x1, local copies, waits for them, and re-layouts, lagrange_section(): node_motion = velocity.reshape(81, zone_count)  1.54 us
  transfers between devices with their start and end apart: 5, of which 2 were waited for; matrix products, arithmetic and copies ran while one was open for 6% of the time, Pallas kernels for 0%

profile of v1, /device:TPU:0, one launch (start us, length us, event | category | flops | bytes accessed | tf_op | source)
XLA Modules:
  0.0 76.2 jit_solution(15084756391232173261)
XLA Ops:
  0.6 1.0 %fusion.62 = (f32[1,2,2,2,4,8,128]{6,5,4,3,2,1,0:T(8,128)S(1)}, f32[1,2,2,2,4,8,128]{6,5,4,3,2,1,0:T(8,128)S(1)}) fusion(f32[2,2,2,2,4,8,128]{6,5,4,3,2,1,0:T(8,128)} %param.11), kind=kLoop, calls=%fused_computation.139 | loop fusion | bytes 524288 | tf_op jit(solution)/shard_map/slice | solution.py:90
  1.7 1.5 %reshape.163 = f32[81,4096]{1,0:T(8,128)S(1)} reshape(f32[3,3,3,3,4,8,128]{6,5,4,3,2,1,0:T(8,128)} %param.12) | data formatting | bytes 2654208 | tf_op jit(solution)/shard_map/reshape | solution.py:87
  3.5 0.8 %convolution_multiply_fusion.5 = f32[8,4096]{1,0:T(8,128)S(1)} fusion(f32[8,4096]{1,0:T(8,128)S(1)} %convolution_multiply_fusion.6, f32[8,81]{1,0:T(8,128)S(1)} %copy-done.8, f32[81,4096]{1,0:T(8,128)S(1)} %reshape.163), kind=kOutput, calls=%fused_computation.17 | convolution fusion | flops 31883264 | bytes 1591840 | tf_op jit(solution)/shard_map/dot_general | solution.py:88
  4.9 2.4 %collective-permute-start.2 = (f32[9,4,128]{2,1,0:T(4,128)S(1)}, f32[9,4,128]{2,1,0:T(4,128)S(1)}, u32[]{:S(2)}, u32[]{:S(2)}) collective-permute-start(f32[9,4,128]{2,1,0:T(4,128)S(1)} %pad_maximum_fusion.11), channel_id=1, source_target_pairs={{0,1},{1,2},{2,3},{4,5},{5,6},{6,7},{8,9},{9,10},{10,11},{12,13},{... | collective-permute-start | bytes 55304 | tf_op jit(solution)/shard_map/ppermute | solution.py:17
  7.4 1.3 %collective-permute-start.3 = (f32[9,4,128]{2,1,0:T(4,128)S(1)}, f32[9,4,128]{2,1,0:T(4,128)S(1)}, u32[]{:S(2)}, u32[]{:S(2)}) collective-permute-start(f32[9,4,128]{2,1,0:T(4,128)S(1)} %pad_maximum_fusion.12), channel_id=1, source_target_pairs={{1,0},{2,1},{3,2},{5,4},{6,5},{7,6},{9,8},{10,9},{11,10},{13,12},{... | collective-permute-start | bytes 55304 | tf_op jit(solution)/shard_map/ppermute | solution.py:17
  8.7 4.2 %collective-permute-start = (f32[9,8,128]{2,1,0:T(8,128)S(1)}, f32[9,8,128]{2,1,0:T(8,128)S(1)}, u32[]{:S(2)}, u32[]{:S(2)}) collective-permute-start(f32[9,8,128]{2,1,0:T(8,128)S(1)} %pad_maximum_fusion.9), channel_id=1, source_target_pairs={{0,4},{4,8},{8,12},{12,16},{16,20},{20,24},{24,28},{1,5},{5,9},{9,... | collective-permute-start | bytes 110600 | tf_op jit(solution)/shard_map/ppermute | solution.py:17
  12.9 1.3 %collective-permute-start.1 = (f32[9,8,128]{2,1,0:T(8,128)S(1)}, f32[9,8,128]{2,1,0:T(8,128)S(1)}, u32[]{:S(2)}, u32[]{:S(2)}) collective-permute-start(f32[9,8,128]{2,1,0:T(8,128)S(1)} %pad_maximum_fusion.10), channel_id=1, source_target_pairs={{4,0},{8,4},{12,8},{16,12},{20,16},{24,20},{28,24},{5,1},{9,5},{13... | collective-permute-start | bytes 110600 | tf_op jit(solution)/shard_map/ppermute | solution.py:17
  15.5 0.4 convolution_bitcast_fusion
  16.5 0.3 convolution_multiply_fusion.3
  16.9 0.4 fusion.5
  17.6 0.4 convolution_bitcast_fusion.1
  18.2 0.6 collective-permute-done.1
  19.0 0.4 convolution_bitcast_fusion.2
  19.8 0.5 copy-done.3
  20.2 0.4 fusion.4
  20.6 0.4 fusion.65
  21.4 43.9 %all-reduce.3 = f32[64]{0:T(128)S(1)} all-reduce(f32[64]{0:T(128)S(1)} %dynamic-update-slice), channel_id=2, replica_groups=mesh['px'=8,'py'=4] {'px','py'}, use_global_device_ids=true, to_apply=%add.3 | all-reduce | flops 64 | bytes 512
  65.7 0.6 gather_fusion
  66.4 0.3 fusion.41
  66.7 0.7 copy.106
  67.4 3.5 %all-to-all-start = ((f32[4,4,16,128]{3,1,2,0:T(4,128)}), f32[4,4,16,128]{3,1,2,0:T(4,128)S(1)}, u32[]{:S(2)}, u32[]{:S(2)}) async-start(f32[4,4,16,128]{3,1,2,0:T(4,128)} %copy.106), calls=%async_computation | async-start | bytes 262144 | tf_op jit(solution)/shard_map/all_to_all | solution.py:192
  70.9 0.8 %broadcast_multiply_fusion = f32[2,2,2,2,4,8,128]{6,5,4,3,2,1,0:T(8,128)} fusion(f32[2,2,2,2,4,8,128]{6,5,4,3,2,1,0:T(8,128)S(1)} %bitcast.158, f32[2]{0:T(128)S(1)} %multiply_divide_fusion), kind=kLoop, calls=%fused_computation.78 | loop fusion | flops 65536 | bytes 524296 | tf_op jit(solution)/shard_map/mul | solution.py:175
  71.7 3.8 %all-to-all-done = f32[4,4,16,128]{3,1,2,0:T(4,128)S(1)} async-done(((f32[4,4,16,128]{3,1,2,0:T(4,128)}), f32[4,4,16,128]{3,1,2,0:T(4,128)S(1)}, u32[]{:S(2)}, u32[]{:S(2)}) %all-to-all-start) | async-done | bytes 131104 | tf_op jit(solution)/shard_map/all_to_all | solution.py:192
  75.5 0.7 copy.107
  (98 shorter events, 4.2 us)
Async XLA Ops:
  1.7 1.6 %copy-start.6 = (f32[8,8]{1,0:T(8,128)S(1)}, f32[8,8]{1,0:T(8,128)}, u32[]{:S(2)}) copy-start(f32[8,8]{1,0:T(8,128)} %constant.61.clone) | copy-start | bytes 772
  1.7 1.9 %copy-start.8 = (f32[8,81]{1,0:T(8,128)S(1)}, f32[8,81]{1,0:T(8,128)}, u32[]{:S(2)}) copy-start(f32[8,81]{1,0:T(8,128)} %constant.62.clone) | copy-start | bytes 7780
  3.2 1.1 %copy-start.7 = (f32[8,8]{1,0:T(8,128)S(1)}, f32[8,8]{1,0:T(8,128)}, u32[]{:S(2)}) copy-start(f32[8,8]{1,0:T(8,128)} %constant.64.clone) | copy-start | bytes 772
  3.3 1.4 %copy-start = (f32[3,3,3,3,4,8,128]{6,5,4,3,2,1,0:T(8,128)S(1)}, f32[3,3,3,3,4,8,128]{6,5,4,3,2,1,0:T(8,128)}, u32[]{:S(2)}) copy-start(f32[3,3,3,3,4,8,128]{6,5,4,3,2,1,0:T(8,128)} %param.12) | copy-start | bytes 3981316
  4.8 9.5 %copy-start.10 = (s32[1,8]{1,0:T(1,128)S(1)}, s32[1,8]{1,0:T(1,128)}, u32[]{:S(2)}) copy-start(s32[1,8]{1,0:T(1,128)} %param.14) | copy-start | bytes 100
  4.9 12.4 %collective-permute-start.2 = (f32[9,4,128]{2,1,0:T(4,128)S(1)}, f32[9,4,128]{2,1,0:T(4,128)S(1)}, u32[]{:S(2)}, u32[]{:S(2)}) collective-permute-start(f32[9,4,128]{2,1,0:T(4,128)S(1)} %pad_maximum_fusion.11), channel_id=1, source_target_pairs={{0,1},{1,2},{2,3},{4,5},{5,6},{6,7},{8,9},{9,10},{10,11},{12,13},{... | collective-permute-start | bytes 55304 | tf_op jit(solution)/shard_map/ppermute | solution.py:17
  7.4 10.0 %collective-permute-start.3 = (f32[9,4,128]{2,1,0:T(4,128)S(1)}, f32[9,4,128]{2,1,0:T(4,128)S(1)}, u32[]{:S(2)}, u32[]{:S(2)}) collective-permute-start(f32[9,4,128]{2,1,0:T(4,128)S(1)} %pad_maximum_fusion.12), channel_id=1, source_target_pairs={{1,0},{2,1},{3,2},{5,4},{6,5},{7,6},{9,8},{10,9},{11,10},{13,12},{... | collective-permute-start | bytes 55304 | tf_op jit(solution)/shard_map/ppermute | solution.py:17
  8.7 9.5 %collective-permute-start = (f32[9,8,128]{2,1,0:T(8,128)S(1)}, f32[9,8,128]{2,1,0:T(8,128)S(1)}, u32[]{:S(2)}, u32[]{:S(2)}) collective-permute-start(f32[9,8,128]{2,1,0:T(8,128)S(1)} %pad_maximum_fusion.9), channel_id=1, source_target_pairs={{0,4},{4,8},{8,12},{12,16},{16,20},{20,24},{24,28},{1,5},{5,9},{9,... | collective-permute-start | bytes 110600 | tf_op jit(solution)/shard_map/ppermute | solution.py:17
  12.9 5.9 %collective-permute-start.1 = (f32[9,8,128]{2,1,0:T(8,128)S(1)}, f32[9,8,128]{2,1,0:T(8,128)S(1)}, u32[]{:S(2)}, u32[]{:S(2)}) collective-permute-start(f32[9,8,128]{2,1,0:T(8,128)S(1)} %pad_maximum_fusion.10), channel_id=1, source_target_pairs={{4,0},{8,4},{12,8},{16,12},{20,16},{24,20},{28,24},{5,1},{9,5},{13... | collective-permute-start | bytes 110600 | tf_op jit(solution)/shard_map/ppermute | solution.py:17
  14.3 1.2 %copy-start.1 = (f32[4,4,1]{1,0,2:T(4,128)S(1)}, f32[4,4,1]{1,0,2:T(4,128)}, u32[]{:S(2)}) copy-start(f32[4,4,1]{1,0,2:T(4,128)} %constant.90) | copy-start | bytes 196
  14.4 1.9 %copy-start.9 = (s32[1,8,1]{1,2,0:T(1,128)S(1)}, s32[1,8,1]{1,2,0:T(1,128)}, u32[]{:S(2)}) copy-start(s32[1,8,1]{1,2,0:T(1,128)} %param.15) | copy-start | bytes 100
  14.6 1.9 %copy-start.5 = (f32[8,8,1]{1,0,2:T(8,128)S(1)}, f32[8,8,1]{1,0,2:T(8,128)}, u32[]{:S(2)}) copy-start(f32[8,8,1]{1,0,2:T(8,128)} %constant.87) | copy-start | bytes 772
  14.9 2.0 %copy-start.4 = (f32[8,8,1]{1,0,2:T(8,128)S(1)}, f32[8,8,1]{1,0,2:T(8,128)}, u32[]{:S(2)}) copy-start(f32[8,8,1]{1,0,2:T(8,128)} %constant.88) | copy-start | bytes 772
  19.5 0.7 copy-start.3
  19.6 1.0 %copy-start.2 = (f32[8,8,1]{1,0,2:T(8,128)S(1)}, f32[8,8,1]{1,0,2:T(8,128)}, u32[]{:S(2)}) copy-start(f32[8,8,1]{1,0,2:T(8,128)} %constant.91) | copy-start | bytes 772
  19.7 45.7 %copy-start.11 = (f32[2]{0:T(128)S(1)}, f32[2]{0:T(128)}, u32[]{:S(2)}) copy-start(f32[2]{0:T(128)} %param.13) | copy-start | bytes 28
  67.4 8.1 %all-to-all-start = ((f32[4,4,16,128]{3,1,2,0:T(4,128)}), f32[4,4,16,128]{3,1,2,0:T(4,128)S(1)}, u32[]{:S(2)}, u32[]{:S(2)}) async-start(f32[4,4,16,128]{3,1,2,0:T(4,128)} %copy.106), calls=%async_computation | async-start | bytes 262144 | tf_op jit(solution)/shard_map/all_to_all | solution.py:192
